TPU v7x, 32 devices: a whole 2x2x4 slice. The times are simulated.
32 devices in a mesh: dp: 4 (over x, core), expert: 8 (over z, y).
Axes of the slice: x: 2, y: 2, z: 4, core: 2. Of those that a mesh axis runs over, the one named last changes fastest.
Arguments:
- dense_weights: bfloat16 [3, 5632, 2048], P(None, 'dp', 'expert'), may hold values from -0.125 to 0.125
- tokens: bfloat16 [1024, 2048], P('expert'), may hold values from -6 to 6
- cotangent: bfloat16 [1024, 2048], P('expert'), may hold values from -6 to 6
- routes: int32 [1024, 4], P('expert'), may hold values from 0 to 7, all different within a row; in each aligned block of 128 rows (0 to 127, 128 to 255, ...) at most 80 rows name the same one
- route_gates: float32 [1024, 4], P('expert'), may hold values from 0.2 to 1
- unit_perm: int32 [2, 5632], replicated, may hold values from 0 to 5631, as said below
- slab_owner: int32 [8], replicated, may hold values from 0 to 7, each once
Outputs:
- mixed: bfloat16 [1024, 2048], P('expert', 'dp')
- token_grad: bfloat16 [1024, 2048], P('expert', 'dp')
- expert_grad: bfloat16 [8, 3, 1408, 2048], P('expert', None, 'dp')
Inputs may be any that keep to these rules, and one draw needn't show every extreme that they name: `unit_perm`: each row is a permutation of the 5632 units. In every row, for every slab s and share g, the 352 positions s * 1408 + g * 352 up to s * 1408 + (g + 1) * 352 - 1 hold exactly 88 units of each block of 1408 consecutive units. `slab_owner`: each slab number c * 4 + s is owned by exactly one expert. `routes`: each row names 4 different experts. In each aligned block of 128 rows no expert is named more than 80 times, a bound that some block reaches.
All inputs are finite; a program needn't handle non-finite values.
Results may differ from a plain program's by a relative error of at most 0.013.
Values may be sent and summed in bfloat16 or wider, within the bound.
A program may use at most 128 MiB of HBM per device.

v0:
```python
import jax
import jax.numpy as jnp
from jax import lax
from jax.sharding import PartitionSpec as P

FF = 5632
EH = 1408


def silu_parts(preact):
    sigmoid_value = jax.nn.sigmoid(preact)
    return (preact * sigmoid_value, sigmoid_value * (1.0 + preact * (1.0 - sigmoid_value)))


def contract_last(left_side, right_side):
    return lax.dot_general(
        left_side, right_side, (((1,), (1,)), ((), ())), preferred_element_type=jnp.float32
    )


def contract_first(left_side, right_side):
    return lax.dot_general(
        left_side, right_side, (((0,), (0,)), ((), ())), preferred_element_type=jnp.float32
    )


def widen_rounded(values):
    return lax.optimization_barrier(values).astype(jnp.float32)


def body(dense_weights, tokens, cotangent, routes, route_gates, unit_perm, slab_owner):
    dp_count = lax.axis_size("dp")
    expert_count = lax.axis_size("expert")
    my_row = lax.axis_index("dp")
    my_col = lax.axis_index("expert")
    block_weights = lax.all_gather(dense_weights, "expert", axis=2, tiled=True)
    block_units = block_weights.shape[1]
    units_share = EH // dp_count
    pick_count = units_share // dp_count
    slab_count = FF // EH
    owned_slab = slab_owner[my_col]
    copy_id = owned_slab // slab_count
    slab_start = owned_slab % slab_count * EH
    shares = lax.dynamic_slice(unit_perm, (copy_id, slab_start), (1, EH)).reshape(
        dp_count, units_share
    )
    sort_order = jnp.argsort(shares // block_units, axis=1, stable=True)
    ordered = jnp.take_along_axis(shares, sort_order, axis=1).reshape(
        dp_count, dp_count, pick_count
    )
    my_units = lax.dynamic_index_in_dim(ordered, my_row, 1, keepdims=False) - my_row * block_units
    outgoing = jnp.take(block_weights, my_units.reshape(-1), axis=1)
    arrived = lax.all_to_all(outgoing, "dp", split_axis=1, concat_axis=1, tiled=True)
    my_order = lax.dynamic_index_in_dim(sort_order, my_row, 0, keepdims=False)
    expert_weights = jnp.take(arrived, jnp.argsort(my_order), axis=1)
    tok_rows = tokens.shape[0]
    route_count = routes.shape[1]
    copies = tok_rows * route_count
    capacity = copies * 5 // (4 * expert_count)
    flat_routes = routes.reshape(-1)
    onehot = (flat_routes[:, None] == jnp.arange(expert_count, dtype=jnp.int32)[None, :]).astype(
        jnp.int32
    )
    slot_rank = jnp.sum((jnp.cumsum(onehot, axis=0) - 1) * onehot, axis=1)
    slot_index = flat_routes * capacity + slot_rank
    source = (
        jnp.full((expert_count * capacity,), copies, jnp.int32)
        .at[slot_index]
        .set(jnp.arange(copies, dtype=jnp.int32))
    )
    filled = source < copies
    safe_rows = jnp.minimum(source, copies - 1)
    token_of = safe_rows // route_count
    pick_rows = jnp.where(filled, token_of, tok_rows)
    padded_tokens = jnp.concatenate([tokens, jnp.zeros((1, tokens.shape[1]), jnp.bfloat16)], axis=0)
    gate_of = jnp.where(filled, route_gates.reshape(-1)[safe_rows], jnp.zeros((), jnp.float32))
    send_x = padded_tokens[pick_rows]
    send_dy = (gate_of[:, None] * cotangent[token_of].astype(jnp.float32)).astype(jnp.bfloat16)
    recv_x, recv_dy = (
        lax.all_to_all(send_x, "expert", split_axis=0, concat_axis=0, tiled=True),
        lax.all_to_all(send_dy, "expert", split_axis=0, concat_axis=0, tiled=True),
    )
    w_gate = expert_weights[0]
    w_up = expert_weights[1]
    w_down = expert_weights[2]
    pre_gate = contract_last(recv_x, w_gate)
    pre_up = contract_last(recv_x, w_up)
    activation, silu_slope = silu_parts(pre_gate)
    hidden = (activation * pre_up).astype(jnp.bfloat16)
    out_part = jnp.dot(hidden, w_down, preferred_element_type=jnp.float32).astype(jnp.bfloat16)
    d_hidden = contract_last(recv_dy, w_down)
    d_gate = (d_hidden * pre_up * silu_slope).astype(jnp.bfloat16)
    d_up = (d_hidden * activation).astype(jnp.bfloat16)
    both_grads = jnp.concatenate([d_gate, d_up], axis=1)
    both_rows = jnp.concatenate([w_gate, w_up], axis=0)
    back_part = jnp.dot(both_grads, both_rows, preferred_element_type=jnp.float32).astype(
        jnp.bfloat16
    )
    weight_grads = jnp.stack(
        [
            contract_first(d_gate, recv_x),
            contract_first(d_up, recv_x),
            contract_first(hidden, recv_dy),
        ]
    ).astype(jnp.bfloat16)[None]
    shared_gate_w = block_weights[0]
    shared_up_w = block_weights[1]
    shared_down_w = block_weights[2]
    shared_gate = contract_last(tokens, shared_gate_w)
    shared_up = contract_last(tokens, shared_up_w)
    shared_act, shared_slope = silu_parts(shared_gate)
    shared_hidden = (shared_act * shared_up).astype(jnp.bfloat16)
    shared_out = jnp.dot(shared_hidden, shared_down_w, preferred_element_type=jnp.float32)
    shared_dh = contract_last(cotangent, shared_down_w)
    shared_dgate = (shared_dh * shared_up * shared_slope).astype(jnp.bfloat16)
    shared_dup = (shared_dh * shared_act).astype(jnp.bfloat16)
    shared_back = jnp.dot(
        shared_dgate, shared_gate_w, preferred_element_type=jnp.float32
    ) + jnp.dot(shared_dup, shared_up_w, preferred_element_type=jnp.float32)
    summed_out, summed_back = (
        lax.psum_scatter(
            widen_rounded(out_part).astype(jnp.bfloat16), "dp", scatter_dimension=1, tiled=True
        ).astype(jnp.float32),
        lax.psum_scatter(
            widen_rounded(back_part).astype(jnp.bfloat16), "dp", scatter_dimension=1, tiled=True
        ).astype(jnp.float32),
    )
    ret_out, ret_back = (
        lax.all_to_all(
            summed_out.astype(jnp.bfloat16), "expert", split_axis=0, concat_axis=0, tiled=True
        ).astype(summed_out.dtype),
        lax.all_to_all(
            summed_back.astype(jnp.bfloat16), "expert", split_axis=0, concat_axis=0, tiled=True
        ).astype(summed_back.dtype),
    )
    rows_out = ret_out[slot_index].reshape(tok_rows, route_count, -1)
    rows_back = ret_back[slot_index].reshape(tok_rows, route_count, -1)
    shared_slice, shared_grad = (
        lax.psum_scatter(
            shared_out.astype(jnp.bfloat16), "dp", scatter_dimension=1, tiled=True
        ).astype(jnp.float32),
        lax.psum_scatter(
            shared_back.astype(jnp.bfloat16), "dp", scatter_dimension=1, tiled=True
        ).astype(jnp.float32),
    )
    mixed = shared_slice + jnp.sum(route_gates[:, :, None] * rows_out, axis=1)
    token_grad = shared_grad + jnp.sum(rows_back, axis=1)
    return (mixed.astype(jnp.bfloat16), token_grad.astype(jnp.bfloat16), weight_grads)


def solution(mesh):
    in_specs = (
        P(None, "dp", "expert"),
        P("expert", None),
        P("expert", None),
        P("expert", None),
        P("expert", None),
        P(),
        P(),
    )
    out_specs = (P("expert", "dp"), P("expert", "dp"), P("expert", None, "dp", None))
    return jax.shard_map(body, mesh=mesh, in_specs=in_specs, out_specs=out_specs, check_vma=False)
```

profile of v0, /device:TPU:0, one launch (start us, length us, event | category | flops | bytes accessed | tf_op | source)
XLA Modules:
  0.0 804.3 jit_solution(1391486535818355225)
XLA Ops:
  7.2 12.2 %copy.24 = bf16[3,1408,256]{2,0,1:T(4,128)(2,1)} copy(bf16[3,1408,256]{2,1,0:T(8,128)(2,1)} %param.7) | data formatting | bytes 4325376 | tf_op args[0]
  21.8 2.4 scatter_custom_fusion
  24.3 4.3 gather_fusion.4
  28.7 4.1 gather_fusion
  32.9 7.8 all-to-all-start
  44.8 3.9 sort.34
  48.8 11.9 %gather_fusion.7 = s32[1408]{0:T(1024)S(1)} fusion(s32[4,352]{1,0:T(4,128)S(1)} %reshape.187, s32[1408]{0:T(1024)S(1)} %reshape.251), kind=kCustom, calls=%fused_computation.7 | custom fusion | bytes 22528 | tf_op jit(solution)/shard_map/jit(take_along_axis)/gather | solution.py:48
  62.3 430.4 %all-gather.2.cloned.1.call-done = bf16[3,1408,2048]{2,0,1:T(4,128)(2,1)} async-done(((bf16[3,1408,256]{2,0,1:T(4,128)(2,1)}), bf16[3,1408,2048]{2,0,1:T(4,128)(2,1)}) %all-gather.2.cloned.1.call-update) | async-done | bytes 17301520 | tf_op jit(solution)/shard_map/all_gather | solution.py:36
  492.7 21.0 %gather_fusion.1 = bf16[352,3,2048]{2,1,0:T(4,128)(2,1)} fusion(bf16[3,1408,2048]{2,0,1:T(4,128)(2,1)} %all-gather.2.cloned.1.call-done, s32[1024]{0:T(1024)S(1)} %pad_clamp_fusion.4), kind=kCustom, calls=%fused_computation.1 | custom fusion | bytes 8652160 | tf_op jit(solution)/shard_map/jit(_take)/gather | solution.py:52
  513.7 7.9 select_bitcast_fusion.1
  521.5 1.5 copy-done.3
  523.0 5.1 all-to-all-start.1
  528.3 3.4 gather_fusion.5
  531.7 2.0 fusion.12
  533.7 59.6 %all-to-all-done.1 = bf16[3,352,2048]{2,0,1:T(4,128)(2,1)} async-done(((bf16[3,352,2048]{2,0,1:T(4,128)(2,1)}), bf16[3,352,2048]{2,0,1:T(4,128)(2,1)}, u32[]{:S(2)}, u32[]{:S(2)}) %all-to-all-start.1) | async-done | bytes 4325408 | tf_op jit(solution)/shard_map/all_to_all | solution.py:53
  593.2 4.6 all-to-all-start.3
  598.4 3.8 sort.35
  602.2 16.0 %gather_fusion.2 = bf16[352,3,2048]{2,1,0:T(4,128)(2,1)} fusion(bf16[3,352,2048]{2,0,1:T(4,128)(2,1)} %all-to-all-done.1, s32[1024]{0:T(1024)S(1)} %pad_clamp_fusion.3), kind=kCustom, calls=%fused_computation.2 | custom fusion | bytes 8652160 | tf_op jit(solution)/shard_map/jit(_take)/gather | solution.py:55
  618.3 5.4 select_bitcast_fusion
  623.7 6.4 fusion.61
  630.9 2.0 copy.71
  633.7 2.3 fusion.62
  636.0 21.1 %all-to-all-done.3 = bf16[8,80,2048]{2,1,0:T(8,128)(2,1)} async-done(((bf16[8,80,2048]{2,1,0:T(8,128)(2,1)}), bf16[8,80,2048]{2,1,0:T(8,128)(2,1)}, u32[]{:S(2)}, u32[]{:S(2)}) %all-to-all-start.3) | async-done | bytes 2621472 | tf_op jit(solution)/shard_map/all_to_all | solution.py:81
  657.1 3.7 fusion.34
  660.9 2.5 multiply_convert_fusion.1
  664.2 3.2 convolution_convert_fusion.1
  667.5 5.8 convolution_convert_fusion
  673.4 43.0 %fusion.60 = (bf16[1,1408,2048]{2,0,1:T(2,128)(2,1)}, bf16[1,1408,2048]{2,0,1:T(2,128)(2,1)}, bf16[1,1408,2048]{2,0,1:T(2,128)(2,1)}) fusion(bf16[3,1408,2048]{2,0,1:T(4,128)(2,1)} %all-gather.2.cloned.1.call-done), kind=kLoop, calls=%fused_computation.121 | loop fusion | bytes 34603008 | tf_op jit(solution)/shard_map/slice | solution.py:106
  716.4 8.5 %fusion.10 = f32[128,1408]{1,0:T(8,128)S(1)} fusion(bf16[128,2048]{1,0:T(8,128)(2,1)S(1)} %copy-done.11, bf16[1,1408,2048]{2,0,1:T(2,128)(2,1)} %get-tuple-element.11), kind=kOutput, calls=%fused_computation.19 | convolution fusion | flops 738197504 | bytes 7012352 | tf_op jit(solution)/shard_map/dot_general | solution.py:16
  724.9 8.1 %fusion = f32[128,1408]{1,0:T(8,128)S(1)} fusion(bf16[128,2048]{1,0:T(8,128)(2,1)S(1)} %copy-done, bf16[1,1408,2048]{2,0,1:T(2,128)(2,1)} %get-tuple-element.12), kind=kOutput, calls=%fused_computation.9 | convolution fusion | flops 738197504 | bytes 7012352 | tf_op jit(solution)/shard_map/dot_general | solution.py:16
  733.0 3.7 fusion.6
  736.7 4.1 fusion.4
  740.9 4.6 fusion.22
  745.6 4.2 all-to-all-start.2
  749.8 8.9 %fusion.25 = bf16[128,2048]{1,0:T(8,128)(2,1)} fusion(bf16[1,1408,2048]{2,0,1:T(2,128)(2,1)} %get-tuple-element.12, f32[128,1408]{1,0:T(8,128)S(1)} %fusion.6, f32[128,1408]{1,0:T(8,128)S(1)} %fusion.10), kind=kOutput, calls=%fused_computation.39 | convolution fusion | flops 739540992 | bytes 7733248 | tf_op jit(solution)/shard_map/dot_general | solution.py:113
  758.8 4.4 fusion.18
  763.2 3.1 all-to-all-done.2
  766.4 4.4 all-to-all-start.4
  770.8 2.4 fusion.16
  773.2 1.3 fusion.17
  774.5 2.3 pad_maximum_fusion
  778.1 1.6 gather_fusion.3
  781.0 6.5 all-to-all-done.4
  788.8 1.6 gather_fusion.6
  790.5 1.3 reshape.191
  791.8 1.8 reduce_sum.32
  794.4 1.6 add_convert_fusion
  796.0 1.6 add_convert_fusion.1
  (108 shorter events, 13.6 us)
Async XLA Ops:
  7.2 521.1 %copy-start = (bf16[128,2048]{1,0:T(8,128)(2,1)S(1)}, bf16[128,2048]{1,0:T(8,128)(2,1)}, u32[]{:S(2)}) copy-start(bf16[128,2048]{1,0:T(8,128)(2,1)} %param.9) | copy-start | bytes 1572868
  7.2 12.3 %copy-start.12 = (s32[128,4]{0,1:T(4,128)S(1)}, s32[128,4]{0,1:T(4,128)}, u32[]{:S(2)}) copy-start(s32[128,4]{0,1:T(4,128)} %param.10) | copy-start | bytes 6148
  7.2 12.9 %copy-start.13 = (f32[128,4]{0,1:T(4,128)S(1)}, f32[128,4]{0,1:T(4,128)}, u32[]{:S(2)}) copy-start(f32[128,4]{0,1:T(4,128)} %param.11) | copy-start | bytes 6148
  7.2 485.5 %all-gather.2.cloned.1.call-start = ((), (), s32[]{:S(2)}) async-start(), calls=%async_computation.9 | async-start | bytes 25952256 | tf_op jit(solution)/shard_map/all_gather | solution.py:36
  19.5 9.1 %copy-start.10 = (bf16[128,2048]{1,0:T(8,128)(2,1)S(1)}, bf16[128,2048]{1,0:T(8,128)(2,1)}, u32[]{:S(2)}) copy-start(bf16[128,2048]{1,0:T(8,128)(2,1)} %param.8) | copy-start | bytes 1572868
  32.9 7.8 copy-start.14
  32.9 488.7 %all-to-all-start = ((bf16[8,80,2048]{2,1,0:T(8,128)(2,1)}), bf16[8,80,2048]{2,1,0:T(8,128)(2,1)S(1)}, u32[]{:S(2)}, u32[]{:S(2)}) async-start(bf16[8,80,2048]{2,1,0:T(8,128)(2,1)} %bitcast.87), calls=%async_computation.1 | async-start | bytes 5242880 | tf_op jit(solution)/shard_map/all_to_all | solution.py:80
  521.5 1.5 copy-start.3
  523.0 70.2 %all-to-all-start.1 = ((bf16[3,352,2048]{2,0,1:T(4,128)(2,1)}), bf16[3,352,2048]{2,0,1:T(4,128)(2,1)}, u32[]{:S(2)}, u32[]{:S(2)}) async-start(bf16[3,352,2048]{2,0,1:T(4,128)(2,1)} %select_bitcast_fusion.1), calls=%async_computation.2 | async-start | bytes 11534336 | tf_op jit(solution)/shard_map/all_to_all | solution.py:53
  593.2 63.9 %all-to-all-start.3 = ((bf16[8,80,2048]{2,1,0:T(8,128)(2,1)}), bf16[8,80,2048]{2,1,0:T(8,128)(2,1)}, u32[]{:S(2)}, u32[]{:S(2)}) async-start(bf16[8,80,2048]{2,1,0:T(8,128)(2,1)} %fusion.12), calls=%async_computation.6 | async-start | bytes 5242880 | tf_op jit(solution)/shard_map/all_to_all | solution.py:81
  597.8 147.8 %reduce-scatter.7.cloned.1.call-start = ((), (), s32[]{:S(2)}) async-start(), calls=%async_computation.11 | async-start | bytes 3276800 | tf_op jit(solution)/shard_map/reduce_scatter | solution.py:121
  630.9 2.0 copy-start.7
  630.9 2.8 copy-start.4
  657.1 3.7 copy-start.5
  657.1 3.7 copy-start.8
  657.1 3.7 copy-start.17
  663.4 0.8 copy-start.15
  667.5 95.8 %reduce-scatter.11.cloned.1.call-start = ((), (), s32[]{:S(2)}) async-start(), calls=%async_computation.13 | async-start | bytes 3276800 | tf_op jit(solution)/shard_map/reduce_scatter | solution.py:124
  673.4 43.0 %copy-start.11 = (bf16[128,2048]{1,0:T(8,128)(2,1)S(1)}, bf16[128,2048]{1,0:T(8,128)(2,1)}, u32[]{:S(2)}) copy-start(bf16[128,2048]{1,0:T(8,128)(2,1)} %param.8) | copy-start | bytes 1572868
  673.4 121.0 %reduce-scatter.9.cloned.1.call-start = ((), (), s32[]{:S(2)}) async-start(), calls=%async_computation.12 | async-start | bytes 655360 | tf_op jit(solution)/shard_map/reduce_scatter | solution.py:142
  716.4 16.6 %copy-start.1 = (bf16[1,1408,2048]{2,0,1:T(2,128)(2,1)S(1)}, bf16[1,1408,2048]{2,0,1:T(2,128)(2,1)}, u32[]{:S(2)}) copy-start(bf16[1,1408,2048]{2,0,1:T(2,128)(2,1)} %get-tuple-element.13) | copy-start | bytes 17301508
  724.9 16.0 %slice-start = ((s8[11534336]{0:T(1024)(128)(4,1)}), s8[3145728]{0:T(1024)(128)(4,1)S(1)}, s32[]{:S(2)}) async-start(s8[11534336]{0:T(1024)(128)(4,1)} %bitcast.85), calls=%async_computation.14 | async-start | bytes 6291456
  733.0 7.8 slice-start.1
  736.7 4.1 slice-start.2
  745.6 20.8 %all-to-all-start.2 = ((bf16[8,80,512]{2,1,0:T(8,128)(2,1)}), bf16[8,80,512]{2,1,0:T(8,128)(2,1)}, u32[]{:S(2)}, u32[]{:S(2)}) async-start(bf16[8,80,512]{2,1,0:T(8,128)(2,1)} %bitcast.98), calls=%async_computation.4 | async-start | bytes 1310720 | tf_op jit(solution)/shard_map/all_to_all | solution.py:129
  749.8 46.2 %reduce-scatter.5.cloned.1.call-start = ((), (), s32[]{:S(2)}) async-start(), calls=%async_computation.10 | async-start | bytes 655360 | tf_op jit(solution)/shard_map/reduce_scatter | solution.py:139
  758.8 12.0 %copy-start.6 = (bf16[8,80,2048]{2,1,0:T(8,128)(2,1)S(1)}, bf16[8,80,2048]{2,1,0:T(8,128)(2,1)}, u32[]{:S(2)}) copy-start(bf16[8,80,2048]{2,1,0:T(8,128)(2,1)} %copy-done.3) | copy-start | bytes 7864324
  766.4 21.2 %all-to-all-start.4 = ((bf16[8,80,512]{2,1,0:T(8,128)(2,1)}), bf16[8,80,512]{2,1,0:T(8,128)(2,1)}, u32[]{:S(2)}, u32[]{:S(2)}) async-start(bf16[8,80,512]{2,1,0:T(8,128)(2,1)} %bitcast.97), calls=%async_computation.8 | async-start | bytes 1310720 | tf_op jit(solution)/shard_map/all_to_all | solution.py:132
  770.8 2.4 copy-start.16
  773.1 1.4 copy-start.9
  790.4 3.2 copy-start.2
Sparse Core Ops, SparseCore 0:
  19.6 473.0 all-gather.1
  667.6 32.6 reduce-scatter.6
  702.8 34.3 reduce-scatter.10
  745.7 19.4 reduce-scatter.8
  767.5 21.6 reduce-scatter.4
where the time goes:
time: 811 us; the launch traced here: 804 us
  waiting for transfers between devices  521 us (64%)
  local copies, waits for them, and re-layouts  140 us (17%)
  matrix products  63.6 us (8%)
  other arithmetic  35.6 us (4%)
  starting transfers between devices  26.8 us (3%)
  between operations  17.2 us (2%)
    all_gather x1, waiting for transfers between devices, body(): block_weights = lax.all_gather(dense_weights, 'expert', axis=2, tiled=True)  430 us
    all_to_all x1, waiting for transfers between devices, body(): lax.all_to_all(outgoing, 'dp', split_axis=1, concat_axis=1, tiled=True)  59.6 us
    slice x1, local copies, waits for them, and re-layouts, body(): shared_gate_w = block_weights[0]  43 us
    dot_general x6, matrix products, contract_last(): lax.dot_general(left_side, right_side, (((1,), (1,)), ((), ())), preferre...  28.8 us
    all_to_all x1, waiting for transfers between devices, body(): lax.all_to_all(send_dy, 'expert', split_axis=0, concat_axis=0, tiled=True)  21.1 us
    gather x1, local copies, waits for them, and re-layouts, body(): outgoing = jnp.take(block_weights, my_units.reshape(-1), axis=1)  21 us
    unnamed x47, local copies, waits for them, and re-layouts  18.5 us
  transfers between devices with their start and end apart: 10, of which 5 were waited for; matrix products, arithmetic and copies ran while one was open for 26% of the time, Pallas kernels for 0%

commit v1 on v0

--- a/solution.py
+++ b/solution.py
@@ -33,7 +33,8 @@
     expert_count = lax.axis_size("expert")
     my_row = lax.axis_index("dp")
     my_col = lax.axis_index("expert")
-    block_weights = lax.all_gather(dense_weights, "expert", axis=2, tiled=True)
+    shards = lax.all_gather(dense_weights, "expert")
+    block_weights = jnp.concatenate(shards, axis=2)
     block_units = block_weights.shape[1]
     units_share = EH // dp_count
     pick_count = units_share // dp_count

time: 811 us -> 739 us (0.911)
  waiting for transfers between devices: 521 us -> 422 us
  local copies, waits for them, and re-layouts: 140 us -> 186 us
  matrix products: 63.6 us -> 44.3 us
    all_gather x1, waiting for transfers between devices: 430 us -> 320 us  [body(): shards = lax.all_gather(dense_weights, 'expert')]
    reshape x0 -> x2, local copies, waits for them, and re-layouts: none -> 58.3 us  [body(): block_weights = jnp.concatenate(shards, axis=2)]
    slice x1 -> x2, local copies, waits for them, and re-layouts: 43 us -> 22 us  [body(): shared_gate_w = block_weights[0]]
    slice x1 -> x3, local copies, waits for them, and re-layouts: 0.21 us -> 17.2 us  [the longest x1 8.66 us: body(): shared_up_w = block_weights[1]]
    dot_general x6, matrix products: 28.8 us -> 14.4 us  [contract_last(): lax.dot_general(left_side, right_side, (((1,), (1,)), ((), ())), preferre...]
    reduce_scatter x1, waiting for transfers between devices: 0.02 us -> 10.1 us  [body(): lax.psum_scatter(shared_back.astype(jnp.bfloat16), 'dp', scatter_dimensio...]
    unnamed x47 -> x38, local copies, waits for them, and re-layouts: 18.5 us -> 9.8 us
  transfers between devices with their start and end apart: 10 -> 10, of which waited for: 5 -> 6; matrix products, arithmetic and copies ran while one was open for 26% -> 34% of each run, Pallas kernels for 0% -> 0%
where the time goes in v1:
time: 739 us; the launch traced here: 733 us
  waiting for transfers between devices  422 us (57%)
  local copies, waits for them, and re-layouts  186 us (25%)
  matrix products  44.3 us (6%)
  other arithmetic  36.3 us (5%)
  starting transfers between devices  26.9 us (4%)
  between operations  17.2 us (2%)
    all_gather x1, waiting for transfers between devices, body(): shards = lax.all_gather(dense_weights, 'expert')  320 us
    all_to_all x1, waiting for transfers between devices, body(): lax.all_to_all(outgoing, 'dp', split_axis=1, concat_axis=1, tiled=True)  59.6 us
    reshape x2, local copies, waits for them, and re-layouts, body(): block_weights = jnp.concatenate(shards, axis=2)  58.3 us
    slice x2, local copies, waits for them, and re-layouts, body(): shared_gate_w = block_weights[0]  22 us
    all_to_all x1, waiting for transfers between devices, body(): lax.all_to_all(send_dy, 'expert', split_axis=0, concat_axis=0, tiled=True)  21.4 us
    gather x1, local copies, waits for them, and re-layouts, body(): outgoing = jnp.take(block_weights, my_units.reshape(-1), axis=1)  20.9 us
    gather x1, local copies, waits for them, and re-layouts, body(): expert_weights = jnp.take(arrived, jnp.argsort(my_order), axis=1)  16 us
  transfers between devices with their start and end apart: 10, of which 6 were waited for; matrix products, arithmetic and copies ran while one was open for 34% of the time, Pallas kernels for 0%

profile of v1, /device:TPU:0, one launch (start us, length us, event | category | flops | bytes accessed | tf_op | source)
XLA Modules:
  0.0 732.6 jit_solution(6725091540916594899)
XLA Ops:
  12.3 2.4 scatter_custom_fusion
  14.8 4.3 gather_fusion.4
  19.2 4.1 gather_fusion
  23.3 8.0 %all-to-all-start = ((bf16[8,80,2048]{2,1,0:T(8,128)(2,1)}), bf16[8,80,2048]{2,1,0:T(8,128)(2,1)S(1)}, u32[]{:S(2)}, u32[]{:S(2)}) async-start(bf16[8,80,2048]{2,1,0:T(8,128)(2,1)} %bitcast.86), calls=%async_computation.1 | async-start | bytes 5242880 | tf_op jit(solution)/shard_map/all_to_all | solution.py:81
  35.5 3.9 sort.34
  39.5 11.9 %gather_fusion.7 = s32[1408]{0:T(1024)S(1)} fusion(s32[4,352]{1,0:T(4,128)S(1)} %reshape.200, s32[1408]{0:T(1024)S(1)} %reshape.265), kind=kCustom, calls=%fused_computation.7 | custom fusion | bytes 22528 | tf_op jit(solution)/shard_map/jit(take_along_axis)/gather | solution.py:49
  52.9 320.3 %all-gather.3.cloned.1.call-done = bf16[24,1408,256]{2,1,0:T(8,128)(2,1)} async-done(((bf16[3,1408,256]{2,1,0:T(8,128)(2,1)}), bf16[24,1408,256]{2,1,0:T(8,128)(2,1)}) %all-gather.3.cloned.1.call-update) | async-done | bytes 17301520 | tf_op jit(solution)/shard_map/all_gather | solution.py:36
  373.3 20.9 %copy.35 = bf16[3,1408,8,256]{1,3,2,0:T(8,128)(2,1)} copy(bf16[3,1408,8,256]{3,1,0,2:T(8,128)(2,1)} %bitcast.78) | data formatting | bytes 34603008 | tf_op jit(solution)/shard_map/reshape | solution.py:37
  394.2 37.4 %copy.36 = bf16[3,1408,2048]{2,0,1:T(4,128)(2,1)} copy(bf16[3,1408,2048]{1,2,0:T(8,128)(2,1)} %bitcast.77) | data formatting | bytes 34603008 | tf_op jit(solution)/shard_map/reshape | solution.py:37
  431.6 20.9 %gather_fusion.1 = bf16[352,3,2048]{2,1,0:T(4,128)(2,1)} fusion(bf16[3,1408,2048]{2,0,1:T(4,128)(2,1)} %copy.36, s32[1024]{0:T(1024)S(1)} %pad_clamp_fusion.4), kind=kCustom, calls=%fused_computation.1 | custom fusion | bytes 8652160 | tf_op jit(solution)/shard_map/jit(_take)/gather | solution.py:53
  452.5 7.9 %select_bitcast_fusion.1 = bf16[3,352,2048]{2,0,1:T(4,128)(2,1)} fusion(bf16[352,3,2048]{2,1,0:T(4,128)(2,1)} %gather_fusion.1, pred[352]{0:T(512)(128)(4,1)S(1)} %compare_and_fusion), kind=kLoop, calls=%fused_computation.10 | loop fusion | flops 2162688 | bytes 8651104 | tf_op jit(solution)/shard_map/jit(_take)/select_n | solution.py:53
  461.9 5.1 all-to-all-start.1
  467.1 3.4 gather_fusion.5
  470.6 2.0 fusion
  472.5 59.6 %all-to-all-done.1 = bf16[3,352,2048]{2,0,1:T(4,128)(2,1)} async-done(((bf16[3,352,2048]{2,0,1:T(4,128)(2,1)}), bf16[3,352,2048]{2,0,1:T(4,128)(2,1)}, u32[]{:S(2)}, u32[]{:S(2)}) %all-to-all-start.1) | async-done | bytes 4325408 | tf_op jit(solution)/shard_map/all_to_all | solution.py:54
  532.1 4.6 all-to-all-start.3
  536.9 3.8 sort.35
  540.7 16.0 %gather_fusion.2 = bf16[352,3,2048]{2,1,0:T(4,128)(2,1)} fusion(bf16[3,352,2048]{2,0,1:T(4,128)(2,1)} %all-to-all-done.1, s32[1024]{0:T(1024)S(1)} %pad_clamp_fusion.3), kind=kCustom, calls=%fused_computation.2 | custom fusion | bytes 8652160 | tf_op jit(solution)/shard_map/jit(_take)/gather | solution.py:56
  556.8 5.4 select_bitcast_fusion
  562.2 6.4 fusion.36
  569.5 2.0 copy.52
  572.3 2.3 fusion.39
  574.5 21.4 %all-to-all-done.3 = bf16[8,80,2048]{2,1,0:T(8,128)(2,1)} async-done(((bf16[8,80,2048]{2,1,0:T(8,128)(2,1)}), bf16[8,80,2048]{2,1,0:T(8,128)(2,1)}, u32[]{:S(2)}, u32[]{:S(2)}) %all-to-all-start.3) | async-done | bytes 2621472 | tf_op jit(solution)/shard_map/all_to_all | solution.py:82
  596.0 3.7 fusion.8
  599.7 2.5 multiply_convert_fusion.1
  603.1 3.2 convolution_convert_fusion.1
  606.4 5.8 convolution_convert_fusion
  612.2 13.8 %fusion.35 = (bf16[1,1408,8,256]{3,1,0,2:T(8,128)(2,1)}, bf16[1,1408,8,256]{3,1,0,2:T(8,128)(2,1)}, bf16[1,1408,8,256]{3,1,0,2:T(8,128)(2,1)}) fusion(bf16[3,1408,8,256]{3,1,0,2:T(8,128)(2,1)} %bitcast.79), kind=kLoop, calls=%fused_computation.104 | loop fusion | bytes 34603008 | tf_op jit(solution)/shard_map/slice | solution.py:107
  626.0 8.2 %copy.28 = bf16[1,1408,8,256]{1,3,2,0:T(8,128)(2,1)} copy(bf16[1,1408,8,256]{3,1,0,2:T(8,128)(2,1)} %get-tuple-element.11) | data formatting | bytes 11534336 | tf_op jit(solution)/shard_map/slice | solution.py:107
  634.2 8.4 %copy.30 = bf16[1,1408,8,256]{1,3,2,0:T(8,128)(2,1)} copy(bf16[1,1408,8,256]{3,1,0,2:T(8,128)(2,1)} %get-tuple-element.12) | data formatting | bytes 11534336 | tf_op jit(solution)/shard_map/slice | solution.py:109
  642.6 8.7 %copy.29 = bf16[1,1408,8,256]{1,3,2,0:T(8,128)(2,1)} copy(bf16[1,1408,8,256]{3,1,0,2:T(8,128)(2,1)} %get-tuple-element.13) | data formatting | bytes 11534336 | tf_op jit(solution)/shard_map/slice | solution.py:108
  651.3 3.8 fusion.37
  656.6 1.6 copy-done.1
  659.3 2.8 convolution_convert_fusion.5
  662.1 4.3 all-to-all-start.2
  666.5 4.6 fusion.18
  671.1 5.5 fusion.7
  676.6 4.4 fusion.6
  681.0 3.1 all-to-all-done.2
  684.1 4.5 all-to-all-start.4
  688.7 2.4 fusion.4
  692.4 2.3 pad_maximum_fusion
  695.9 1.6 gather_fusion.3
  698.9 6.8 all-to-all-done.4
  706.9 1.6 gather_fusion.6
  709.9 1.9 reduce_sum.32
  712.5 1.6 add_convert_fusion.1
  714.1 10.1 %reduce-scatter.9.cloned.1.call-done = bf16[128,512]{1,0:T(8,128)(2,1)} async-done(((bf16[128,2048]{1,0:T(8,128)(2,1)}), bf16[128,512]{1,0:T(8,128)(2,1)}) %reduce-scatter.9.cloned.1.call-update) | async-done | bytes 131088 | tf_op jit(solution)/shard_map/reduce_scatter | solution.py:143
  (103 shorter events, 24.2 us)
Async XLA Ops:
  7.2 460.0 %copy-start = (bf16[128,2048]{1,0:T(8,128)(2,1)S(1)}, bf16[128,2048]{1,0:T(8,128)(2,1)}, u32[]{:S(2)}) copy-start(bf16[128,2048]{1,0:T(8,128)(2,1)} %param.9) | copy-start | bytes 1572868
  7.2 366.1 %all-gather.3.cloned.1.call-start = ((), (), s32[]{:S(2)}) async-start(), calls=%async_computation.13 | async-start | bytes 19464192 | tf_op jit(solution)/shard_map/all_gather | solution.py:36
  7.9 11.2 %copy-start.3 = (bf16[128,2048]{1,0:T(8,128)(2,1)S(1)}, bf16[128,2048]{1,0:T(8,128)(2,1)}, u32[]{:S(2)}) copy-start(bf16[128,2048]{1,0:T(8,128)(2,1)} %param.8) | copy-start | bytes 1572868
  23.3 8.0 %copy-start.13 = (s32[8]{0:T(128)S(1)}, s32[8]{0:T(128)}, u32[]{:S(2)}) copy-start(s32[8]{0:T(128)} %param.13) | copy-start | bytes 100
  23.3 437.1 %all-to-all-start = ((bf16[8,80,2048]{2,1,0:T(8,128)(2,1)}), bf16[8,80,2048]{2,1,0:T(8,128)(2,1)S(1)}, u32[]{:S(2)}, u32[]{:S(2)}) async-start(bf16[8,80,2048]{2,1,0:T(8,128)(2,1)} %bitcast.86), calls=%async_computation.1 | async-start | bytes 5242880 | tf_op jit(solution)/shard_map/all_to_all | solution.py:81
  460.4 1.5 copy-start.6
  461.9 70.2 %all-to-all-start.1 = ((bf16[3,352,2048]{2,0,1:T(4,128)(2,1)}), bf16[3,352,2048]{2,0,1:T(4,128)(2,1)}, u32[]{:S(2)}, u32[]{:S(2)}) async-start(bf16[3,352,2048]{2,0,1:T(4,128)(2,1)} %select_bitcast_fusion.1), calls=%async_computation.2 | async-start | bytes 11534336 | tf_op jit(solution)/shard_map/all_to_all | solution.py:54
  532.1 63.9 %all-to-all-start.3 = ((bf16[8,80,2048]{2,1,0:T(8,128)(2,1)}), bf16[8,80,2048]{2,1,0:T(8,128)(2,1)}, u32[]{:S(2)}, u32[]{:S(2)}) async-start(bf16[8,80,2048]{2,1,0:T(8,128)(2,1)} %fusion), calls=%async_computation.6 | async-start | bytes 5242880 | tf_op jit(solution)/shard_map/all_to_all | solution.py:82
  536.7 125.4 %reduce-scatter.7.cloned.1.call-start = ((), (), s32[]{:S(2)}) async-start(), calls=%async_computation.10 | async-start | bytes 3276800 | tf_op jit(solution)/shard_map/reduce_scatter | solution.py:122
  569.5 2.0 copy-start.10
  569.5 2.8 copy-start.7
  596.0 3.7 copy-start.8
  596.0 3.7 copy-start.11
  596.0 3.7 copy-start.16
  602.3 0.8 copy-start.14
  606.3 74.7 %reduce-scatter.11.cloned.1.call-start = ((), (), s32[]{:S(2)}) async-start(), calls=%async_computation.12 | async-start | bytes 3276800 | tf_op jit(solution)/shard_map/reduce_scatter | solution.py:125
  612.2 100.3 %reduce-scatter.5.cloned.1.call-start = ((), (), s32[]{:S(2)}) async-start(), calls=%async_computation.9 | async-start | bytes 655360 | tf_op jit(solution)/shard_map/reduce_scatter | solution.py:140
  642.6 8.7 %copy-start.4 = (bf16[128,2048]{1,0:T(8,128)(2,1)S(1)}, bf16[128,2048]{1,0:T(8,128)(2,1)}, u32[]{:S(2)}) copy-start(bf16[128,2048]{1,0:T(8,128)(2,1)} %param.8) | copy-start | bytes 1572868
  651.3 4.3 copy-start.2
  655.6 2.6 copy-start.1
  662.1 22.0 %all-to-all-start.2 = ((bf16[8,80,512]{2,1,0:T(8,128)(2,1)}), bf16[8,80,512]{2,1,0:T(8,128)(2,1)}, u32[]{:S(2)}, u32[]{:S(2)}) async-start(bf16[8,80,512]{2,1,0:T(8,128)(2,1)} %bitcast.97), calls=%async_computation.4 | async-start | bytes 1310720 | tf_op jit(solution)/shard_map/all_to_all | solution.py:130
  666.5 57.7 %reduce-scatter.9.cloned.1.call-start = ((), (), s32[]{:S(2)}) async-start(), calls=%async_computation.11 | async-start | bytes 655360 | tf_op jit(solution)/shard_map/reduce_scatter | solution.py:143
  676.6 12.0 %copy-start.9 = (bf16[8,80,2048]{2,1,0:T(8,128)(2,1)S(1)}, bf16[8,80,2048]{2,1,0:T(8,128)(2,1)}, u32[]{:S(2)}) copy-start(bf16[8,80,2048]{2,1,0:T(8,128)(2,1)} %copy-done.6) | copy-start | bytes 7864324
  684.1 21.5 %all-to-all-start.4 = ((bf16[8,80,512]{2,1,0:T(8,128)(2,1)}), bf16[8,80,512]{2,1,0:T(8,128)(2,1)}, u32[]{:S(2)}, u32[]{:S(2)}) async-start(bf16[8,80,512]{2,1,0:T(8,128)(2,1)} %bitcast.96), calls=%async_computation.8 | async-start | bytes 1310720 | tf_op jit(solution)/shard_map/all_to_all | solution.py:133
  688.6 2.4 copy-start.15
  691.0 1.4 copy-start.12
  708.5 3.2 copy-start.5
Sparse Core Ops, SparseCore 0:
  9.5 363.7 all-gather.2
  606.4 32.6 reduce-scatter.6
  641.7 34.3 reduce-scatter.10
  678.5 21.6 reduce-scatter.4
  702.5 21.6 reduce-scatter.8
